TPU v7x, 256 devices: a whole 4x4x8 slice. The times are simulated.
256 devices in a mesh: row: 8 (over x, core), col: 32 (over y, z).
Axes of the slice: x: 4, y: 4, z: 8, core: 2. Of those that a mesh axis runs over, the one named last changes fastest.
Arguments:
- deflation: bfloat16 [16, 256, 16, 3072], P('row', 'col'), may hold values from 0 to 0.019897461
- coefficient: float32 [16, 256, 16], P('row', 'col'), may hold values from 1 to 10
- gradients: bfloat16 [3, 64, 64], replicated, may hold values from -0.75 to 0.75
- x_penalty: float32 [24, 256, 16], P('row', 'col'), may hold values from 1 to 10, as said below
- y_penalty: float32 [16, 288, 16], P('row', 'col'), may hold values from 1 to 10, as said below
- z_penalty: float32 [16, 256, 17], P('row', 'col'), may hold values from 1 to 10
- coarse_order: int32 [1024], replicated, may hold values from 0 to 1023, as said below
Outputs:
- coarse_blocks: float32 [1024, 7, 2304], P(('row', 'col'))
- panel: float32 [1024, 48, 528], P(('row', 'col'))
Inputs may be any that keep to these rules, and one draw needn't show every extreme that they name: `coarse_order`: each subdomain number appears once; subdomains with consecutive coarse numbers are mostly neighbours along the third or second dimension. `x_penalty`: row i * 3 + 2 equals row (i + 1) * 3: a face between two devices' blocks is held by both. `y_penalty`: column j * 9 + 8 equals column (j + 1) * 9: a face between two devices' blocks is held by both.
All inputs are finite; a program needn't handle non-finite values.
Results may differ from a plain program's by a relative error of at most 0.00044.
Values may be sent and summed in bfloat16 or wider, within the bound.
No kernel may reach another device: no remote copies, remote signals or barrier semaphores. Data moves between devices by JAX's collectives and lax.ppermute only.
A program may use at most 128 MiB of HBM per device.

v0:
```python
import jax
import jax.numpy as jnp
from jax import lax
from jax.sharding import PartitionSpec as P

NV = 48
SUB_DEV = 4
PB = 11
LINE_WEIGHTS = (1.0 / 6.0, 5.0 / 6.0, 5.0 / 6.0, 1.0 / 6.0)


def with_halo(shard, sides, width):
    for axis, dim in sides:
        size, length = (lax.axis_size(axis), shard.shape[dim])
        up = [(i, (i + 1) % size) for i in range(size - 1)]
        down = [(j, i) for i, j in up]
        last = lax.slice_in_dim(shard, length - width, length, axis=dim)
        initial = lax.slice_in_dim(shard, 0, width, axis=dim)
        before = lax.ppermute(last, axis, up)
        after = lax.ppermute(initial, axis, down)
        shard = jnp.concatenate([before, shard, after], axis=dim)
    return shard


def node_weights():
    line = jnp.array(LINE_WEIGHTS, jnp.float32)
    return (line[:, None, None] * line[None, :, None] * line[None, None, :]).reshape(64)


def contract(form, left, right):
    return jnp.einsum(form, left, right, preferred_element_type=jnp.float32)


def traces(values, axis, side):
    lead = values.ndim - 1
    nodes = values.reshape(values.shape[:lead] + (4, 4, 4, NV))
    picked = lax.index_in_dim(nodes, side, lead + axis, keepdims=False)
    return picked.reshape(values.shape[:lead] + (16, NV))


def scaled(trace, root):
    return (root[..., None, None] * trace.astype(jnp.float32)).astype(jnp.bfloat16)


def grouped(left, right, groups):
    shape = left.shape
    split = shape[:2] + (groups, shape[2] // groups) + shape[3:]
    return contract("xyskav,xyskaw->svw", left.reshape(split), right.reshape(split))


def lateral(plus, minus, root, below, above, groups):
    jump = (
        root[1:-1, :, :, None, None]
        * (plus[:-1].astype(jnp.float32) - minus[1:].astype(jnp.float32))
    ).astype(jnp.bfloat16)
    low_own = scaled(minus[0], root[0])
    low_other = scaled(below, root[0])
    high_own = scaled(plus[-1], root[-1])
    high_other = scaled(above, root[-1])
    self_part = (
        grouped(jump, jump, groups)
        + grouped(low_own[None], low_own[None], groups)
        + grouped(high_own[None], high_own[None], groups)
    )
    return (
        self_part,
        -grouped(low_own[None], low_other[None], groups),
        -grouped(high_own[None], high_other[None], groups),
    )


def vertical(plus, minus, root, groups):
    width, length, depth = plus.shape[:3]
    height = depth // groups
    plus = plus.reshape(width, length, groups, height, 16, NV)
    minus = minus.reshape(width, length, groups, height, 16, NV)
    inner_root = root[:, :, :depth].reshape(width, length, groups, height)[:, :, :, 1:]
    jump = (
        inner_root[..., None, None]
        * (plus[:, :, :, :-1].astype(jnp.float32) - minus[:, :, :, 1:].astype(jnp.float32))
    ).astype(jnp.bfloat16)
    edge_root = root[:, :, ::height]
    first = minus[:, :, :, 0]
    last = plus[:, :, :, -1]
    blank = jnp.zeros_like(last[:, :, :1])
    low_own = scaled(first, edge_root[:, :, :groups])
    low_other = scaled(jnp.concatenate([blank, last[:, :, :-1]], axis=2), edge_root[:, :, :groups])
    high_own = scaled(last, edge_root[:, :, 1:])
    high_other = scaled(jnp.concatenate([first[:, :, 1:], blank], axis=2), edge_root[:, :, 1:])
    pairing = "xysav,xysaw->svw"
    self_part = (
        contract("xyskav,xyskaw->svw", jump, jump)
        + contract(pairing, low_own, low_own)
        + contract(pairing, high_own, high_own)
    )
    return (
        self_part,
        -contract(pairing, low_own, low_other),
        -contract(pairing, high_own, high_other),
    )


def volume(values, coefficient, gradients, groups):
    width, length, depth = values.shape[:3]
    nodes = values.reshape(width, length, depth, 64, NV)
    factor = jnp.sqrt(coefficient[..., None] * node_weights())
    total = jnp.zeros((groups, NV, NV), jnp.float32)
    for axis in range(3):
        product = contract("ab,xyzbv->xyzav", gradients[axis], nodes)
        rounded = (product * factor[..., None]).astype(jnp.bfloat16)
        rounded = rounded.reshape(width, length, groups, depth // groups, 64, NV)
        total = total + contract("xyskav,xyskaw->svw", rounded, rounded)
    return total


def panel_rows(blocks, column_block, present):
    picks = (
        present[:, :, None]
        & (column_block[:, :, None] == jnp.arange(PB, dtype=jnp.int32)[None, None, :])
    ).astype(jnp.float32)
    rows = jnp.einsum("stp,stvw->svpw", picks, blocks, precision=lax.Precision.HIGHEST).reshape(
        blocks.shape[0], NV, PB * NV
    )
    select = (column_block[:, :1] == jnp.arange(PB, dtype=jnp.int32)[None, :]).astype(jnp.float32)
    share = jnp.einsum("sp,svq->pvq", select, rows, precision=lax.Precision.HIGHEST)
    return (rows, select, share)


def finish(rows, select, assembled):
    whole = assembled.reshape(PB * NV, PB * NV)
    factor = jnp.linalg.cholesky(0.5 * (whole + whole.T))
    count = rows.shape[0]
    solved = jax.scipy.linalg.solve_triangular(
        factor, rows.reshape(count * NV, PB * NV).T, lower=True
    ).T.reshape(count, NV, PB * NV)
    inside = jnp.einsum(
        "sp,pvq->svq", select, factor.reshape(PB, NV, PB * NV), precision=lax.Precision.HIGHEST
    )
    return jnp.where(jnp.sum(select, axis=1)[:, None, None] > 0, inside, solved)


def shards(deflation, coefficient, gradients, x_penalty, y_penalty, z_penalty, coarse_order):
    plus_x = traces(deflation, 0, 3)
    minus_x = traces(deflation, 0, 0)
    plus_y = traces(deflation, 1, 3)
    minus_y = traces(deflation, 1, 0)
    padded = with_halo(deflation, (("row", 0), ("col", 1)), 1)
    below_x = traces(padded[0, 1:-1], 0, 3)
    above_x = traces(padded[-1, 1:-1], 0, 0)
    below_y = traces(padded[1:-1, 0], 1, 3)
    above_y = traces(padded[1:-1, -1], 1, 0)
    x_root = jnp.sqrt(x_penalty)
    y_root = jnp.sqrt(y_penalty)
    z_root = jnp.sqrt(z_penalty)
    self_x, low_x, high_x = lateral(plus_x, minus_x, x_root, below_x, above_x, SUB_DEV)
    self_y, low_y, high_y = lateral(
        jnp.swapaxes(plus_y, 0, 1),
        jnp.swapaxes(minus_y, 0, 1),
        jnp.swapaxes(y_root, 0, 1),
        below_y,
        above_y,
        SUB_DEV,
    )
    self_z, low_z, high_z = vertical(
        traces(deflation, 2, 3), traces(deflation, 2, 0), z_root, SUB_DEV
    )
    diagonal = volume(deflation, coefficient, gradients, SUB_DEV) + self_x + self_y + self_z
    blocks = jnp.stack([diagonal, low_x, high_x, low_y, high_y, low_z, high_z], axis=1)
    row_pos = lax.axis_index("row")
    col_pos = lax.axis_index("col")
    row_count = lax.axis_size("row")
    col_count = lax.axis_size("col")
    device = row_pos * col_count + col_pos
    local = jnp.arange(SUB_DEV, dtype=jnp.int32)
    owner = device * SUB_DEV + local
    stride = col_count * SUB_DEV
    neighbours = jnp.stack(
        [
            owner,
            owner - stride,
            owner + stride,
            owner - SUB_DEV,
            owner + SUB_DEV,
            owner - 1,
            owner + 1,
        ],
        axis=1,
    )
    always = jnp.ones((SUB_DEV,), bool)
    present = jnp.stack(
        [
            always,
            always & (row_pos > 0),
            always & (row_pos < row_count - 1),
            always & (col_pos > 0),
            always & (col_pos < col_count - 1),
            local > 0,
            local < SUB_DEV - 1,
        ],
        axis=1,
    )
    match = (
        neighbours[:, :, None] == jnp.arange(coarse_order.shape[0], dtype=jnp.int32)[None, None, :]
    )
    column_block = jnp.sum(jnp.where(match, coarse_order[None, None, :], 0), axis=-1)
    rows, select, share = panel_rows(blocks, column_block, present)
    assembled = lax.psum(share, ("row", "col"))
    panel = finish(rows, select, assembled)
    return (blocks.reshape(SUB_DEV, 7, NV * NV), panel)


def solution(mesh):
    in_specs = (
        P("row", "col", None, None),
        P("row", "col", None),
        P(),
        P("row", "col", None),
        P("row", "col", None),
        P("row", "col", None),
        P(),
    )
    out_specs = (P(("row", "col"), None, None), P(("row", "col"), None, None))
    return jax.shard_map(shards, mesh=mesh, in_specs=in_specs, out_specs=out_specs, check_vma=False)
```

profile of v0, /device:TPU:6, one launch (start us, length us, event | category | flops | bytes accessed | tf_op | source)
XLA Modules:
  0.0 590.4 jit_solution(2413078286542607056)
XLA Ops:
  7.2 2.8 fusion.121
  11.9 3.6 collective-permute-start.1
  15.6 5.4 reshape.330
  21.0 2.6 fusion.118
  23.6 2.6 convert_subtract_fusion
  26.1 4.1 fusion.119
  30.8 5.3 reshape.326
  36.5 5.3 multiply_convert_fusion
  44.0 4.5 fusion.117
  57.8 4.5 convolution_bitcast_fusion.12
  79.9 2.9 copy.249
  86.2 3.1 convolution_bitcast_fusion.1
  89.4 6.7 %reshape_squeeze.26 = bf16[8,16,4,4,4,48]{5,4,3,2,1,0:T(4,128)(2,1)} reshape(bf16[1,8,16,3072]{3,2,1,0:T(8,128)(2,1)} %collective-permute-done) | data formatting | bytes 1572864 | tf_op jit(solution)/shard_map/reshape;squeeze | solution.py:36
  100.9 6.2 %reshape_squeeze.27 = bf16[8,16,4,4,4,48]{5,4,3,2,1,0:T(4,128)(2,1)} reshape(bf16[1,8,16,3072]{3,2,1,0:T(8,128)(2,1)} %collective-permute-done.1) | data formatting | bytes 1572864 | tf_op jit(solution)/shard_map/reshape;squeeze | solution.py:36
  115.0 4.7 collective-permute-start.2
  129.0 3.3 collective-permute-done.3
  145.4 259.5 %all-reduce.7.cloned.1.call-done = f32[528,528]{0,1:T(8,128)} async-done(((f32[528,528]{0,1:T(8,128)}), f32[528,528]{0,1:T(8,128)}) %all-reduce.7.cloned.1.call-update) | async-done | bytes 1115152 | tf_op jit(solution)/shard_map/psum | solution.py:207
  404.9 3.0 copy.282
  411.2 11.9 %cholesky.134 = f32[128,128]{1,0:T(8,128)S(1)} custom-call(f32[128,128]{1,0:T(8,128)S(1)} %cholesky.346), custom_call_target="Cholesky" | custom-call | tf_op jit(solution)/shard_map/jit(cholesky)/cholesky | solution.py:131
  423.2 9.8 %custom-call.39 = f32[1,128,128]{1,2,0:T(8,128)S(1)} custom-call(f32[1,128,128]{2,1,0:T(8,128)S(1)} %get-tuple-element.54), custom_call_target="InvertDiagBlocksLowerTriangular" | custom-call | tf_op jit(solution)/shard_map/jit(cholesky)/cholesky | solution.py:131
  435.6 11.7 %cholesky.274 = f32[128,128]{1,0:T(8,128)S(1)} custom-call(f32[128,128]{1,0:T(8,128)S(1)} %cholesky.350), custom_call_target="Cholesky" | custom-call | tf_op jit(solution)/shard_map/jit(cholesky)/cholesky | solution.py:131
  448.7 9.8 %custom-call.40 = f32[1,128,128]{1,2,0:T(8,128)S(1)} custom-call(f32[1,128,128]{2,1,0:T(8,128)S(1)} %get-tuple-element.51), custom_call_target="InvertDiagBlocksLowerTriangular" | custom-call | tf_op jit(solution)/shard_map/jit(cholesky)/cholesky | solution.py:131
  460.1 12.1 %cholesky.295 = f32[128,128]{1,0:T(8,128)S(1)} custom-call(f32[128,128]{1,0:T(8,128)S(1)} %cholesky.355), custom_call_target="Cholesky" | custom-call | tf_op jit(solution)/shard_map/jit(cholesky)/cholesky | solution.py:131
  472.8 9.8 %custom-call.41 = f32[1,128,128]{1,2,0:T(8,128)S(1)} custom-call(f32[1,128,128]{2,1,0:T(8,128)S(1)} %get-tuple-element.48), custom_call_target="InvertDiagBlocksLowerTriangular" | custom-call | tf_op jit(solution)/shard_map/jit(cholesky)/cholesky | solution.py:131
  484.1 11.7 %cholesky.314 = f32[128,128]{1,0:T(8,128)S(1)} custom-call(f32[128,128]{1,0:T(8,128)S(1)} %cholesky.360), custom_call_target="Cholesky" | custom-call | tf_op jit(solution)/shard_map/jit(cholesky)/cholesky | solution.py:131
  496.5 9.8 %custom-call.42 = f32[1,128,128]{1,2,0:T(8,128)S(1)} custom-call(f32[1,128,128]{2,1,0:T(8,128)S(1)} %get-tuple-element.45), custom_call_target="InvertDiagBlocksLowerTriangular" | custom-call | tf_op jit(solution)/shard_map/jit(cholesky)/cholesky | solution.py:131
  514.0 11.9 %while.1 = (s32[]{:T(128)}, f32[528,528]{1,0:T(8,128)}, s32[4,2]{0,1:T(2,128)S(1)}, f32[4,128,128]{2,1,0:T(8,128)S(1)}, s32[]{:T(128)}) while((s32[]{:T(128)}, f32[528,528]{1,0:T(8,128)}, s32[4,2]{0,1:T(2,128)S(1)}, f32[4,128,128]{2,1,0:T(8,128)S(1)}, s32[]{:T(128)}) %tuple.72), condition=%wide.while_cond, body=%wide.while_body.sunk | while | flops 2 | bytes 131181 | solution.py:133
  514.8 2.3 bitcast_dynamic-update-slice_fusion.9
  517.8 2.3 bitcast_dynamic-update-slice_fusion.9
  520.7 2.3 bitcast_dynamic-update-slice_fusion.9
  523.6 2.3 bitcast_dynamic-update-slice_fusion.9
  526.0 49.1 %custom-call.43 = f32[5,128,128]{1,2,0:T(8,128)S(1)} custom-call(f32[5,128,128]{2,1,0:T(8,128)S(1)} %pad_maximum_fusion), custom_call_target="InvertDiagBlocksLowerTriangular" | custom-call | tf_op jit(solution)/shard_map/jit(_solve_triangular)/triangular_solve | solution.py:133
  (300 shorter events, 96.7 us)
Async XLA Ops:
  7.2 8.4 %copy-start.3 = (bf16[2,8,16,3072]{3,2,1,0:T(8,128)(2,1)S(1)}, bf16[2,8,16,3072]{3,2,1,0:T(8,128)(2,1)}, u32[]{:S(2)}) copy-start(bf16[2,8,16,3072]{3,2,1,0:T(8,128)(2,1)} %param.8) | copy-start | bytes 4718596
  7.2 397.8 %all-reduce.7.cloned.1.call-start = ((), (), s32[]{:S(2)}) async-start(), calls=%async_computation | async-start | bytes 2703360 | tf_op jit(solution)/shard_map/psum | solution.py:207
  10.0 79.4 %collective-permute-start = (bf16[1,8,16,3072]{3,2,1,0:T(8,128)(2,1)}, bf16[1,8,16,3072]{3,2,1,0:T(8,128)(2,1)}, u32[]{:S(2)}, u32[]{:S(2)}) collective-permute-start(bf16[1,8,16,3072]{3,2,1,0:T(8,128)(2,1)} %get-tuple-element.43), channel_id=1, source_target_pairs={{0,32},{32,64},{64,96},{96,128},{128,160},{160,192},{192,224},{1,3... | collective-permute-start | bytes 2359304 | tf_op jit(solution)/shard_map/ppermute | solution.py:19
  11.9 88.9 %collective-permute-start.1 = (bf16[1,8,16,3072]{3,2,1,0:T(8,128)(2,1)}, bf16[1,8,16,3072]{3,2,1,0:T(8,128)(2,1)}, u32[]{:S(2)}, u32[]{:S(2)}) collective-permute-start(bf16[1,8,16,3072]{3,2,1,0:T(8,128)(2,1)} %get-tuple-element.42), channel_id=1, source_target_pairs={{32,0},{64,32},{96,64},{128,96},{160,128},{192,160},{224,192},{33,... | collective-permute-start | bytes 2359304 | tf_op jit(solution)/shard_map/ppermute | solution.py:20
  30.3 5.8 copy-start.36
  30.8 5.3 copy-start.45
  30.8 5.5 copy-start.41
  30.8 5.7 copy-start.35
  36.5 5.3 copy-start
  44.0 8.1 %copy-start.39 = (f32[3,8,16]{2,1,0:T(8,128)S(1)}, f32[3,8,16]{2,1,0:T(8,128)}, u32[]{:S(2)}) copy-start(f32[3,8,16]{2,1,0:T(8,128)} %param.11) | copy-start | bytes 4612
  67.7 4.3 copy-start.57
  67.7 4.3 copy-start.58
  67.7 4.3 copy-start.59
  67.7 4.3 copy-start.60
  67.7 4.3 copy-start.46
  67.7 4.7 copy-start.34
  67.7 6.0 %copy-start.17 = (bf16[1,8,16,1,4,4,48]{6,5,4,3,2,1,0:T(4,128)(2,1)S(1)}, bf16[1,8,16,1,4,4,48]{6,5,4,3,2,1,0:T(4,128)(2,1)}, u32[]{:S(2)}) copy-start(bf16[1,8,16,1,4,4,48]{6,5,4,3,2,1,0:T(4,128)(2,1)} %get-tuple-element.36) | copy-start | bytes 589828
  67.8 6.0 %copy-start.18 = (bf16[1,8,16,1,4,4,48]{6,5,4,3,2,1,0:T(4,128)(2,1)S(1)}, bf16[1,8,16,1,4,4,48]{6,5,4,3,2,1,0:T(4,128)(2,1)}, u32[]{:S(2)}) copy-start(bf16[1,8,16,1,4,4,48]{6,5,4,3,2,1,0:T(4,128)(2,1)} %get-tuple-element.37) | copy-start | bytes 589828
  70.2 5.5 copy-start.15
  70.2 5.8 copy-start.21
  112.8 8.4 %copy-start.20 = (f32[1,8,16,1,4,4,48]{6,1,5,4,2,3,0:T(8,128)S(1)}, f32[1,8,16,1,4,4,48]{6,1,5,4,2,3,0:T(8,128)}, u32[]{:S(2)}) copy-start(f32[1,8,16,1,4,4,48]{6,1,5,4,2,3,0:T(8,128)} %copy.245) | copy-start | bytes 1179652
  112.8 8.4 %copy-start.43 = (f32[1,8,16]{1,2,0:T(8,128)S(1)}, f32[1,8,16]{1,2,0:T(8,128)}, u32[]{:S(2)}) copy-start(f32[1,8,16]{1,2,0:T(8,128)} %get-tuple-element.55) | copy-start | bytes 1540
  112.8 8.4 %copy-start.64 = (f32[4,48,48]{2,1,0:T(8,128)S(1)}, f32[4,48,48]{2,1,0:T(8,128)}, u32[]{:S(2)}) copy-start(f32[4,48,48]{2,1,0:T(8,128)} %convolution_bitcast_fusion.10) | copy-start | bytes 110596
  115.0 6.7 %copy-start.28 = (f32[4,48,48]{2,1,0:T(8,128)S(1)}, f32[4,48,48]{2,1,0:T(8,128)}, u32[]{:S(2)}) copy-start(f32[4,48,48]{2,1,0:T(8,128)} %convolution_bitcast_fusion.12) | copy-start | bytes 110596
  115.0 6.7 %copy-start.29 = (f32[4,48,48]{2,1,0:T(8,128)S(1)}, f32[4,48,48]{2,1,0:T(8,128)}, u32[]{:S(2)}) copy-start(f32[4,48,48]{2,1,0:T(8,128)} %convolution_bitcast_fusion.13) | copy-start | bytes 110596
  115.0 6.7 %copy-start.33 = (f32[4,48,48]{2,1,0:T(8,128)S(1)}, f32[4,48,48]{2,1,0:T(8,128)}, u32[]{:S(2)}) copy-start(f32[4,48,48]{2,1,0:T(8,128)} %fusion.24) | copy-start | bytes 110596
  115.0 12.5 %collective-permute-start.2 = (bf16[4,1,16,3072]{3,2,1,0:T(8,128)(2,1)}, bf16[4,1,16,3072]{3,2,1,0:T(8,128)(2,1)}, u32[]{:S(2)}, u32[]{:S(2)}) collective-permute-start(bf16[4,1,16,3072]{3,2,1,0:T(8,128)(2,1)} %get-tuple-element.41), channel_id=1, source_target_pairs={{0,1},{1,2},{2,3},{3,4},{4,5},{5,6},{6,7},{7,8},{8,9},{9,10},{10,1... | collective-permute-start | bytes 1179656 | tf_op jit(solution)/shard_map/ppermute | solution.py:19
  119.7 12.6 %collective-permute-start.3 = (bf16[4,1,16,3072]{3,2,1,0:T(8,128)(2,1)}, bf16[4,1,16,3072]{3,2,1,0:T(8,128)(2,1)}, u32[]{:S(2)}, u32[]{:S(2)}) collective-permute-start(bf16[4,1,16,3072]{3,2,1,0:T(8,128)(2,1)} %get-tuple-element.40), channel_id=1, source_target_pairs={{1,0},{2,1},{3,2},{4,3},{5,4},{6,5},{7,6},{8,7},{9,8},{10,9},{11,1... | collective-permute-start | bytes 1179656 | tf_op jit(solution)/shard_map/ppermute | solution.py:20
  125.8 8.1 %copy-start.16 = (f32[1,2,16,16,48]{4,2,3,0,1:T(8,128)S(1)}, f32[1,2,16,16,48]{4,2,3,0,1:T(8,128)}, u32[]{:S(2)}) copy-start(f32[1,2,16,16,48]{4,2,3,0,1:T(8,128)} %slice_convert_fusion.1) | copy-start | bytes 294916
  129.0 5.6 slice-start
  512.7 13.2 %copy-start.31 = (f32[128,112]{1,0:T(8,128)S(1)}, f32[128,112]{1,0:T(8,128)}, u32[]{:S(2)}) copy-start(f32[128,112]{1,0:T(8,128)} %pad_convert_fusion) | copy-start | bytes 172036
  576.5 4.8 copy-start.61
  (42 other events, 84.3 us)
Sparse Core Ops, SparseCore 0:
  142.6 262.2 all-reduce.6
where the time goes:
time: 597 us; the launch traced here: 590 us
  waiting for transfers between devices  264 us (44%)
  other arithmetic  157 us (26%)
  local copies, waits for them, and re-layouts  95.1 us (16%)
  matrix products  44.6 us (7%)
  between operations  18.6 us (3%)
  starting transfers between devices  11.8 us (2%)
    psum x1, waiting for transfers between devices, shards(): assembled = lax.psum(share, ('row', 'col'))  259 us
    another operation x19, other arithmetic, finish(): factor = jnp.linalg.cholesky(0.5 * (whole + whole.T))  91.6 us
    another operation x7, other arithmetic, finish(): jax.scipy.linalg.solve_triangular(factor, rows.reshape(count * NV, PB * N...  50.7 us
    dot_general x21, matrix products, contract(): return jnp.einsum(form, left, right, preferred_element_type=jnp.float32)  28.5 us
    slice x10, local copies, waits for them, and re-layouts, traces(): picked = lax.index_in_dim(nodes, side, lead + axis, keepdims=False)  16.6 us
    another operation x4, local copies, waits for them, and re-layouts, traces(): nodes = values.reshape(values.shape[:lead] + (4, 4, 4, NV))  14 us
    unnamed x143, local copies, waits for them, and re-layouts  12.1 us
  transfers between devices with their start and end apart: 5, of which 3 were waited for; matrix products, arithmetic and copies ran while one was open for 15% of the time, Pallas kernels for 0%

commit v1 on v0

--- a/solution.py
+++ b/solution.py
@@ -204,7 +204,9 @@
     )
     column_block = jnp.sum(jnp.where(match, coarse_order[None, None, :], 0), axis=-1)
     rows, select, share = panel_rows(blocks, column_block, present)
-    assembled = lax.psum(share, ("row", "col"))
+    assembled = share
+    for to_i in ("row", "col"):
+        assembled = jax.lax.psum(assembled, axis_name=to_i)
     panel = finish(rows, select, assembled)
     return (blocks.reshape(SUB_DEV, 7, NV * NV), panel)
 

time: 597 us -> 560 us (0.938)
  waiting for transfers between devices: 264 us -> 224 us
    psum x1 -> x2, waiting for transfers between devices: 259 us -> 219 us  [shards(): assembled = jax.lax.psum(assembled, axis_name=to_i)]
    unnamed x143 -> x141, local copies, waits for them, and re-layouts: 12.1 us -> 12 us
  transfers between devices with their start and end apart: 5 -> 6, of which waited for: 3 -> 4; matrix products, arithmetic and copies ran while one was open for 15% -> 17% of each run, Pallas kernels for 0% -> 0%
where the time goes in v1:
time: 560 us; the launch traced here: 553 us
  waiting for transfers between devices  224 us (40%)
  other arithmetic  156 us (28%)
  local copies, waits for them, and re-layouts  96.2 us (17%)
  matrix products  46 us (8%)
  between operations  19 us (3%)
  starting transfers between devices  11.8 us (2%)
    psum x2, waiting for transfers between devices, shards(): assembled = jax.lax.psum(assembled, axis_name=to_i)  219 us
    another operation x19, other arithmetic, finish(): factor = jnp.linalg.cholesky(0.5 * (whole + whole.T))  91.6 us
    another operation x7, other arithmetic, finish(): jax.scipy.linalg.solve_triangular(factor, rows.reshape(count * NV, PB * N...  51.2 us
    dot_general x21, matrix products, contract(): return jnp.einsum(form, left, right, preferred_element_type=jnp.float32)  28.6 us
    slice x10, local copies, waits for them, and re-layouts, traces(): picked = lax.index_in_dim(nodes, side, lead + axis, keepdims=False)  16.5 us
    another operation x4, local copies, waits for them, and re-layouts, traces(): nodes = values.reshape(values.shape[:lead] + (4, 4, 4, NV))  13.9 us
    another operation x13, local copies, waits for them, and re-layouts  12 us
    unnamed x141, local copies, waits for them, and re-layouts  12 us
  transfers between devices with their start and end apart: 6, of which 4 were waited for; matrix products, arithmetic and copies ran while one was open for 17% of the time, Pallas kernels for 0%

profile of v1, /device:TPU:6, one launch (start us, length us, event | category | flops | bytes accessed | tf_op | source)
XLA Modules:
  0.0 552.7 jit_solution(14297277470521270706)
XLA Ops:
  7.2 2.8 fusion.121
  11.9 3.6 collective-permute-start.1
  15.6 5.4 reshape.330
  21.0 2.6 fusion.118
  23.6 2.6 convert_subtract_fusion
  26.1 4.1 fusion.119
  30.3 5.3 reshape.326
  36.0 5.3 multiply_convert_fusion
  43.5 4.5 fusion.117
  56.5 4.4 convolution_bitcast_fusion.12
  78.4 2.9 copy.249
  85.3 3.3 convolution_bitcast_fusion.1
  88.6 6.6 %reshape_squeeze.26 = bf16[8,16,4,4,4,48]{5,4,3,2,1,0:T(4,128)(2,1)} reshape(bf16[1,8,16,3072]{3,2,1,0:T(8,128)(2,1)} %collective-permute-done) | data formatting | bytes 1572864 | tf_op jit(solution)/shard_map/reshape;squeeze | solution.py:36
  99.4 6.2 %reshape_squeeze.27 = bf16[8,16,4,4,4,48]{5,4,3,2,1,0:T(4,128)(2,1)} reshape(bf16[1,8,16,3072]{3,2,1,0:T(8,128)(2,1)} %collective-permute-done.1) | data formatting | bytes 1572864 | tf_op jit(solution)/shard_map/reshape;squeeze | solution.py:36
  112.0 4.7 collective-permute-start.2
  126.0 3.3 collective-permute-done.3
  136.6 2.4 fusion.33
  140.6 68.5 %all-reduce.8.cloned.1.call-done = f32[11,48,528]{2,0,1:T(8,128)} async-done(((f32[11,48,528]{2,0,1:T(8,128)}), f32[11,48,528]{2,0,1:T(8,128)}) %all-reduce.8.cloned.1.call-update) | async-done | bytes 1115152 | tf_op jit(solution)/shard_map/psum | solution.py:209
  216.0 150.6 %all-reduce.10.cloned.1.call-done = f32[528,528]{0,1:T(8,128)} async-done(((f32[528,528]{0,1:T(8,128)}), f32[528,528]{0,1:T(8,128)}) %all-reduce.10.cloned.1.call-update) | async-done | bytes 1115152 | tf_op jit(solution)/shard_map/psum | solution.py:209
  366.6 3.0 copy.282
  372.9 11.7 %cholesky.134 = f32[128,128]{1,0:T(8,128)S(1)} custom-call(f32[128,128]{1,0:T(8,128)S(1)} %cholesky.346), custom_call_target="Cholesky" | custom-call | tf_op jit(solution)/shard_map/jit(cholesky)/cholesky | solution.py:131
  384.7 9.8 %custom-call.39 = f32[1,128,128]{1,2,0:T(8,128)S(1)} custom-call(f32[1,128,128]{2,1,0:T(8,128)S(1)} %get-tuple-element.54), custom_call_target="InvertDiagBlocksLowerTriangular" | custom-call | tf_op jit(solution)/shard_map/jit(cholesky)/cholesky | solution.py:131
  397.1 11.9 %cholesky.274 = f32[128,128]{1,0:T(8,128)S(1)} custom-call(f32[128,128]{1,0:T(8,128)S(1)} %cholesky.350), custom_call_target="Cholesky" | custom-call | tf_op jit(solution)/shard_map/jit(cholesky)/cholesky | solution.py:131
  410.4 9.8 %custom-call.40 = f32[1,128,128]{1,2,0:T(8,128)S(1)} custom-call(f32[1,128,128]{2,1,0:T(8,128)S(1)} %get-tuple-element.51), custom_call_target="InvertDiagBlocksLowerTriangular" | custom-call | tf_op jit(solution)/shard_map/jit(cholesky)/cholesky | solution.py:131
  421.8 11.7 %cholesky.295 = f32[128,128]{1,0:T(8,128)S(1)} custom-call(f32[128,128]{1,0:T(8,128)S(1)} %cholesky.355), custom_call_target="Cholesky" | custom-call | tf_op jit(solution)/shard_map/jit(cholesky)/cholesky | solution.py:131
  434.2 9.8 %custom-call.41 = f32[1,128,128]{1,2,0:T(8,128)S(1)} custom-call(f32[1,128,128]{2,1,0:T(8,128)S(1)} %get-tuple-element.48), custom_call_target="InvertDiagBlocksLowerTriangular" | custom-call | tf_op jit(solution)/shard_map/jit(cholesky)/cholesky | solution.py:131
  445.5 12.0 %cholesky.314 = f32[128,128]{1,0:T(8,128)S(1)} custom-call(f32[128,128]{1,0:T(8,128)S(1)} %cholesky.360), custom_call_target="Cholesky" | custom-call | tf_op jit(solution)/shard_map/jit(cholesky)/cholesky | solution.py:131
  458.2 9.8 %custom-call.42 = f32[1,128,128]{1,2,0:T(8,128)S(1)} custom-call(f32[1,128,128]{2,1,0:T(8,128)S(1)} %get-tuple-element.45), custom_call_target="InvertDiagBlocksLowerTriangular" | custom-call | tf_op jit(solution)/shard_map/jit(cholesky)/cholesky | solution.py:131
  475.8 12.1 %while.1 = (s32[]{:T(128)}, f32[528,528]{1,0:T(8,128)}, s32[4,2]{0,1:T(2,128)S(1)}, f32[4,128,128]{2,1,0:T(8,128)S(1)}, s32[]{:T(128)}) while((s32[]{:T(128)}, f32[528,528]{1,0:T(8,128)}, s32[4,2]{0,1:T(2,128)S(1)}, f32[4,128,128]{2,1,0:T(8,128)S(1)}, s32[]{:T(128)}) %tuple.74), condition=%wide.while_cond, body=%wide.while_body.sunk | while | flops 2 | bytes 131181 | solution.py:133
  476.5 2.3 bitcast_dynamic-update-slice_fusion.9
  479.5 2.3 bitcast_dynamic-update-slice_fusion.9
  488.0 49.1 %custom-call.43 = f32[5,128,128]{1,2,0:T(8,128)S(1)} custom-call(f32[5,128,128]{2,1,0:T(8,128)S(1)} %pad_maximum_fusion), custom_call_target="InvertDiagBlocksLowerTriangular" | custom-call | tf_op jit(solution)/shard_map/jit(_solve_triangular)/triangular_solve | solution.py:133
  (301 shorter events, 101.3 us)
Async XLA Ops:
  7.2 8.4 %copy-start.3 = (bf16[2,8,16,3072]{3,2,1,0:T(8,128)(2,1)S(1)}, bf16[2,8,16,3072]{3,2,1,0:T(8,128)(2,1)}, u32[]{:S(2)}) copy-start(bf16[2,8,16,3072]{3,2,1,0:T(8,128)(2,1)} %param.8) | copy-start | bytes 4718596
  7.2 201.9 %all-reduce.8.cloned.1.call-start = ((), (), s32[]{:S(2)}) async-start(), calls=%async_computation | async-start | bytes 3932160 | tf_op jit(solution)/shard_map/psum | solution.py:209
  10.0 78.6 %collective-permute-start = (bf16[1,8,16,3072]{3,2,1,0:T(8,128)(2,1)}, bf16[1,8,16,3072]{3,2,1,0:T(8,128)(2,1)}, u32[]{:S(2)}, u32[]{:S(2)}) collective-permute-start(bf16[1,8,16,3072]{3,2,1,0:T(8,128)(2,1)} %get-tuple-element.43), channel_id=1, source_target_pairs={{0,32},{32,64},{64,96},{96,128},{128,160},{160,192},{192,224},{1,3... | collective-permute-start | bytes 2359304 | tf_op jit(solution)/shard_map/ppermute | solution.py:19
  11.9 87.4 %collective-permute-start.1 = (bf16[1,8,16,3072]{3,2,1,0:T(8,128)(2,1)}, bf16[1,8,16,3072]{3,2,1,0:T(8,128)(2,1)}, u32[]{:S(2)}, u32[]{:S(2)}) collective-permute-start(bf16[1,8,16,3072]{3,2,1,0:T(8,128)(2,1)} %get-tuple-element.42), channel_id=1, source_target_pairs={{32,0},{64,32},{96,64},{128,96},{160,128},{192,160},{224,192},{33,... | collective-permute-start | bytes 2359304 | tf_op jit(solution)/shard_map/ppermute | solution.py:20
  30.3 5.4 copy-start.35
  30.3 5.3 copy-start.43
  30.3 5.6 %copy-start.40 = (f32[2,8,16]{2,1,0:T(8,128)S(1)}, f32[2,8,16]{2,1,0:T(8,128)}, u32[]{:S(2)}) copy-start(f32[2,8,16]{2,1,0:T(8,128)} %param.9) | copy-start | bytes 3076
  30.3 5.7 %copy-start.34 = (bf16[3,64,64]{2,1,0:T(8,128)(2,1)S(1)}, bf16[3,64,64]{2,1,0:T(8,128)(2,1)}, u32[]{:S(2)}) copy-start(bf16[3,64,64]{2,1,0:T(8,128)(2,1)} %param.10) | copy-start | bytes 73732
  36.0 5.3 copy-start
  43.5 7.9 %copy-start.38 = (f32[3,8,16]{2,1,0:T(8,128)S(1)}, f32[3,8,16]{2,1,0:T(8,128)}, u32[]{:S(2)}) copy-start(f32[3,8,16]{2,1,0:T(8,128)} %param.11) | copy-start | bytes 4612
  66.4 4.3 copy-start.57
  66.4 4.3 copy-start.58
  66.4 4.3 copy-start.59
  66.4 4.3 copy-start.44
  66.4 4.6 copy-start.33
  66.4 5.9 %copy-start.17 = (bf16[1,8,16,1,4,4,48]{6,5,4,3,2,1,0:T(4,128)(2,1)S(1)}, bf16[1,8,16,1,4,4,48]{6,5,4,3,2,1,0:T(4,128)(2,1)}, u32[]{:S(2)}) copy-start(bf16[1,8,16,1,4,4,48]{6,5,4,3,2,1,0:T(4,128)(2,1)} %get-tuple-element.36) | copy-start | bytes 589828
  66.5 5.9 %copy-start.18 = (bf16[1,8,16,1,4,4,48]{6,5,4,3,2,1,0:T(4,128)(2,1)S(1)}, bf16[1,8,16,1,4,4,48]{6,5,4,3,2,1,0:T(4,128)(2,1)}, u32[]{:S(2)}) copy-start(bf16[1,8,16,1,4,4,48]{6,5,4,3,2,1,0:T(4,128)(2,1)} %get-tuple-element.37) | copy-start | bytes 589828
  68.9 5.4 copy-start.15
  68.9 5.7 %copy-start.21 = (bf16[7,2,16,16,48]{4,2,3,0,1:T(8,128)(2,1)S(1)}, bf16[7,2,16,16,48]{4,2,3,0,1:T(8,128)(2,1)}, u32[]{:S(2)}) copy-start(bf16[7,2,16,16,48]{4,2,3,0,1:T(8,128)(2,1)} %multiply_convert_fusion.3) | copy-start | bytes 1032196
  109.7 8.3 %copy-start.20 = (f32[1,8,16,1,4,4,48]{6,1,5,4,2,3,0:T(8,128)S(1)}, f32[1,8,16,1,4,4,48]{6,1,5,4,2,3,0:T(8,128)}, u32[]{:S(2)}) copy-start(f32[1,8,16,1,4,4,48]{6,1,5,4,2,3,0:T(8,128)} %copy.245) | copy-start | bytes 1179652
  109.7 8.3 %copy-start.42 = (f32[1,8,16]{1,2,0:T(8,128)S(1)}, f32[1,8,16]{1,2,0:T(8,128)}, u32[]{:S(2)}) copy-start(f32[1,8,16]{1,2,0:T(8,128)} %get-tuple-element.55) | copy-start | bytes 1540
  112.0 6.5 %copy-start.25 = (f32[4,48,48]{2,1,0:T(8,128)S(1)}, f32[4,48,48]{2,1,0:T(8,128)}, u32[]{:S(2)}) copy-start(f32[4,48,48]{2,1,0:T(8,128)} %convolution_bitcast_fusion.12) | copy-start | bytes 110596
  112.0 6.5 %copy-start.26 = (f32[4,48,48]{2,1,0:T(8,128)S(1)}, f32[4,48,48]{2,1,0:T(8,128)}, u32[]{:S(2)}) copy-start(f32[4,48,48]{2,1,0:T(8,128)} %convolution_bitcast_fusion.13) | copy-start | bytes 110596
  112.0 6.5 %copy-start.32 = (f32[4,48,48]{2,1,0:T(8,128)S(1)}, f32[4,48,48]{2,1,0:T(8,128)}, u32[]{:S(2)}) copy-start(f32[4,48,48]{2,1,0:T(8,128)} %fusion.24) | copy-start | bytes 110596
  112.0 12.5 %collective-permute-start.2 = (bf16[4,1,16,3072]{3,2,1,0:T(8,128)(2,1)}, bf16[4,1,16,3072]{3,2,1,0:T(8,128)(2,1)}, u32[]{:S(2)}, u32[]{:S(2)}) collective-permute-start(bf16[4,1,16,3072]{3,2,1,0:T(8,128)(2,1)} %get-tuple-element.41), channel_id=1, source_target_pairs={{0,1},{1,2},{2,3},{3,4},{4,5},{5,6},{6,7},{7,8},{8,9},{9,10},{10,1... | collective-permute-start | bytes 1179656 | tf_op jit(solution)/shard_map/ppermute | solution.py:19
  116.7 12.6 %collective-permute-start.3 = (bf16[4,1,16,3072]{3,2,1,0:T(8,128)(2,1)}, bf16[4,1,16,3072]{3,2,1,0:T(8,128)(2,1)}, u32[]{:S(2)}, u32[]{:S(2)}) collective-permute-start(bf16[4,1,16,3072]{3,2,1,0:T(8,128)(2,1)} %get-tuple-element.40), channel_id=1, source_target_pairs={{1,0},{2,1},{3,2},{4,3},{5,4},{6,5},{7,6},{8,7},{9,8},{10,9},{11,1... | collective-permute-start | bytes 1179656 | tf_op jit(solution)/shard_map/ppermute | solution.py:20
  121.8 9.0 %copy-start.16 = (f32[1,2,16,16,48]{4,2,3,0,1:T(8,128)S(1)}, f32[1,2,16,16,48]{4,2,3,0,1:T(8,128)}, u32[]{:S(2)}) copy-start(f32[1,2,16,16,48]{4,2,3,0,1:T(8,128)} %slice_convert_fusion.1) | copy-start | bytes 294916
  125.9 5.6 %slice-start = ((bf16[2,8,4,16,48]{4,1,3,2,0:T(8,128)(2,1)}), bf16[2,8,3,16,48]{4,1,3,2,0:T(8,128)(2,1)S(1)}, s32[]{:S(2)}) async-start(bf16[2,8,4,16,48]{4,1,3,2,0:T(8,128)(2,1)} %slice_bitcast_fusion), calls=%async_computation.2 | async-start | bytes 393216 | tf_op jit(solution)/shard_map/slice | solution.py:87
  126.0 5.6 %copy-start.48 = (f32[2,8,4]{1,2,0:T(4,128)S(1)}, f32[2,8,4]{1,2,0:T(4,128)}, u32[]{:S(2)}) copy-start(f32[2,8,4]{1,2,0:T(4,128)} %get-tuple-element.66) | copy-start | bytes 772
  139.0 227.6 %all-reduce.10.cloned.1.call-start = ((), (), s32[]{:S(2)}) async-start(), calls=%async_computation.1 | async-start | bytes 2703360 | tf_op jit(solution)/shard_map/psum | solution.py:209
  474.5 13.4 %copy-start.28 = (f32[128,112]{1,0:T(8,128)S(1)}, f32[128,112]{1,0:T(8,128)}, u32[]{:S(2)}) copy-start(f32[128,112]{1,0:T(8,128)} %pad_convert_fusion) | copy-start | bytes 172036
  538.5 4.8 copy-start.60
  (42 other events, 87.1 us)
Sparse Core Ops, SparseCore 0:
  139.1 69.9 all-reduce.7
  212.8 153.7 all-reduce.9
